TPU v7x, 32 devices: a whole 2x2x4 slice. The times are simulated.
32 devices in a mesh: sec: 4 (over z), tile: 4 (over y, core), role: 2 (over x).
Axes of the slice: x: 2, y: 2, z: 4, core: 2. Of those that a mesh axis runs over, the one named last changes fastest.
Arguments:
- pressure: float32 [32, 256, 8192], P(None, 'sec', ('tile', 'role')), may hold values from -6 to 6
- cell_weight: float32 [8192], P(('tile', 'role')), may hold values from 0.25 to 4
- live_cells: int32 [8], replicated, may hold values from 341 to 1024, as said below
- mode_order: int32 [128], replicated, may hold values from 0 to 127, each once
Outputs:
- gram: float32 [128, 32, 32], P('sec', ('tile', 'role'))
Inputs may be any that keep to these rules, and one draw needn't show every extreme that they name: `live_cells`: at least one tile half is full. `mode_order`: each wavenumber appears once.
All inputs are finite; a program needn't handle non-finite values.
Results may differ from a plain program's by a relative error of at most 0.0003.
Values sent between devices are 32-bit elements; how exact they have to be, the bound alone decides.
A program may use at most 128 MiB of HBM per device.

v0:
```python
import math
import jax
import jax.numpy as jnp
from jax import lax
from jax.sharding import PartitionSpec as P


def time_table(count):
    steps = jnp.arange(count, dtype=jnp.int32)
    half = count // 2
    freqs = jnp.arange(half, dtype=jnp.int32)
    hann = 0.5 - 0.5 * jnp.cos(2.0 * math.pi * steps.astype(jnp.float32) / count)
    phase = 2.0 * math.pi * (freqs[:, None] * steps[None, :] % count).astype(jnp.float32) / count
    factor = math.sqrt(8.0 / (3.0 * count))
    return jnp.concatenate(
        [factor * hann[None, :] * jnp.cos(phase), -factor * hann[None, :] * jnp.sin(phase)], axis=0
    )


def angle_table(mode_order, angles):
    index = jnp.arange(angles, dtype=jnp.int32)
    phase = (
        2.0 * math.pi * (mode_order[:, None] * index[None, :] % angles).astype(jnp.float32) / angles
    )
    cosine = jnp.cos(phase) / math.sqrt(angles)
    sine = jnp.sin(phase) / math.sqrt(angles)
    return jnp.stack(
        [jnp.stack([cosine, sine], axis=1), jnp.stack([-sine, cosine], axis=1)], axis=0
    )


def on_device(pressure, cell_weight, live_cells, mode_order):
    hi = lax.Precision.HIGHEST
    snaps = pressure.shape[0]
    half = snaps // 2
    n_sec = lax.axis_size("sec")
    n_grp = lax.axis_size("tile") * lax.axis_size("role")
    angles = pressure.shape[1] * n_sec
    group_cells = pressure.shape[2]
    cell_dev = group_cells // n_sec
    modes = mode_order.shape[0]
    total_cells = group_cells * n_grp
    htab = time_table(snaps)
    atab = angle_table(mode_order, angles)
    arrived = lax.all_to_all(pressure, "sec", split_axis=2, concat_axis=1, tiled=True)
    spectra = jnp.einsum("rt,tqc->rqc", htab, arrived, precision=hi)
    split = spectra.reshape(2, half, angles, cell_dev)
    modal = jnp.einsum("okiq,ifqc->kofc", atab, split, precision=hi).reshape(modes, snaps, cell_dev)
    group = lax.axis_index("tile") * lax.axis_size("role") + lax.axis_index("role")
    live = lax.dynamic_slice_in_dim(live_cells, group, 1, 0)[0]
    owned = lax.all_to_all(modal, "sec", split_axis=0, concat_axis=2, tiled=True)
    position = jnp.arange(group_cells, dtype=jnp.int32)
    weighted = jnp.where(position < live, cell_weight / total_cells, jnp.float32(0.0))
    local_gram = jnp.einsum("kac,kbc->kab", owned * weighted[None, None, :], owned, precision=hi)
    result = lax.psum_scatter(local_gram, ("tile", "role"), scatter_dimension=1, tiled=True)
    return result


def solution(mesh):
    in_specs = (P(None, "sec", ("tile", "role")), P(("tile", "role")), P(), P())
    out_specs = P("sec", ("tile", "role"), None)
    return jax.shard_map(
        on_device, mesh=mesh, in_specs=in_specs, out_specs=out_specs, check_vma=False
    )
```

profile of v0, /device:TPU:0, one launch (start us, length us, event | category | flops | bytes accessed | tf_op | source)
XLA Modules:
  0.0 474.0 jit_solution(6145706416273522948)
XLA Ops:
  6.5 16.2 %copy.12 = f32[32,64,1024]{1,0,2:T(8,128)} copy(f32[32,64,1024]{2,1,0:T(8,128)} %param.4) | data formatting | bytes 16777216 | tf_op args[0]
  22.7 14.4 %reshape.145 = f32[4,1,524288]{2,1,0:T(1,128)} reshape(f32[1024,32,64]{2,1,0:T(8,128)} %bitcast.38) | data formatting | bytes 16777216
  37.1 6.5 %all-to-all-start = ((f32[4,1,524288]{2,1,0:T(1,128)}), f32[4,1,524288]{2,1,0:T(1,128)}, u32[]{:S(2)}, u32[]{:S(2)}) async-start(f32[4,1,524288]{2,1,0:T(1,128)} %reshape.145), calls=%async_computation | async-start | bytes 16777216 | tf_op jit(solution)/shard_map/all_to_all | solution.py:45
  43.7 0.1 sine_multiply_fusion.1
  43.8 0.6 sine_multiply_fusion
  44.4 183.2 %all-to-all-done = f32[4,1,524288]{2,1,0:T(1,128)} async-done(((f32[4,1,524288]{2,1,0:T(1,128)}), f32[4,1,524288]{2,1,0:T(1,128)}, u32[]{:S(2)}, u32[]{:S(2)}) %all-to-all-start) | async-done | bytes 8388640 | tf_op jit(solution)/shard_map/all_to_all | solution.py:45
  227.7 0.5 broadcast.237
  228.2 28.8 %reduce = f32[4,524288]{1,0:T(4,128)} reduce(f32[4,1,524288]{2,1,0:T(1,128)} %all-to-all-done, f32[]{:T(128)} %broadcast.237), dimensions={1}, to_apply=%all_to_all.26.reduce_sub_computation | reduce | bytes 16777220 | tf_op jit(solution)/shard_map/all_to_all | solution.py:45
  256.9 16.8 %reshape.146 = f32[1024,32,64]{2,1,0:T(8,128)} reshape(f32[4,524288]{1,0:T(4,128)} %reduce) | data formatting | bytes 16777216
  273.7 13.2 %copy.24 = f32[32,64,4,256]{3,2,1,0:T(4,128)} copy(f32[32,64,4,256]{1,0,3,2:T(8,128)} %bitcast.37) | data formatting | bytes 16777216 | tf_op jit(solution)/shard_map/all_to_all | solution.py:45
  286.9 8.2 %copy.25 = f32[32,4,64,256]{3,0,2,1:T(8,128)S(1)} copy(f32[32,4,64,256]{3,1,2,0:T(4,128)} %bitcast.40) | data formatting | bytes 16777216 | tf_op jit(solution)/shard_map/all_to_all | solution.py:45
  295.1 8.4 %convolution_bitcast_fusion = f32[2,16,256,256,1]{3,1,2,0,4:T(8,128)S(1)} fusion(f32[2,16,32,1]{2,1,3,0:T(8,128)S(1)} %bitcast.43, f32[32,256,256,1]{2,0,1,3:T(8,128)S(1)} %bitcast.41), kind=kOutput, calls=%fused_computation.4 | convolution fusion | flops 805306368 | bytes 16781312 | tf_op jit(solution)/shard_map/rt,tqc->rqc/dot_general | solution.py:46
  303.5 17.4 %fusion.4 = f32[128,2,16,256]{0,3,1,2:T(8,128)} fusion(f32[2,16,256,256,1]{3,1,2,0,4:T(8,128)S(1)} %convolution_bitcast_fusion, f32[1,128,2,256]{3,1,2,0:T(8,128)S(1)} %get-tuple-element.6, f32[1,128,2,256]{3,1,2,0:T(8,128)S(1)} %get-tuple-element.5), kind=kOutput, calls=%fused_computation.5 | convolution fusion | flops 6442582016 | bytes 13107200 | tf_op jit(solution)/shard_map/okiq,ifqc->kofc/dot_general | solution.py:48
  320.9 5.5 %copy.17 = f32[128,2,16,256]{3,2,1,0:T(8,128)} copy(f32[128,2,16,256]{0,3,1,2:T(8,128)} %fusion.4) | data formatting | bytes 8388608 | tf_op jit(solution)/shard_map/okiq,ifqc->kofc/transpose | solution.py:48
  326.5 4.8 %all-to-all-start.1 = ((f32[128,32,256]{2,1,0:T(8,128)}), f32[128,32,256]{2,1,0:T(8,128)}, u32[]{:S(2)}, u32[]{:S(2)}) async-start(f32[128,32,256]{2,1,0:T(8,128)} %bitcast.42), calls=%async_computation.1 | async-start | bytes 8388608 | tf_op jit(solution)/shard_map/all_to_all | solution.py:51
  331.3 0.3 reduce-scatter.2.cloned.1.call-start
  331.7 0.6 dynamic_slice.3
  332.2 0.6 multiply_select_fusion
  332.9 91.3 %all-to-all-done.1 = f32[128,32,256]{2,1,0:T(8,128)} async-done(((f32[128,32,256]{2,1,0:T(8,128)}), f32[128,32,256]{2,1,0:T(8,128)}, u32[]{:S(2)}, u32[]{:S(2)}) %all-to-all-start.1) | async-done | bytes 4194336 | tf_op jit(solution)/shard_map/all_to_all | solution.py:51
  424.2 2.7 copy.28
  426.9 4.1 fusion.2
  431.0 1.1 copy.19
  432.1 33.2 %reduce-scatter.2.cloned.1.call-done = f32[32,4,32]{2,0,1:T(8,128)} async-done(((f32[32,32,32]{2,0,1:T(8,128)}), f32[32,4,32]{2,0,1:T(8,128)}) %reduce-scatter.2.cloned.1.call-update) | async-done | bytes 16400 | tf_op jit(solution)/shard_map/reduce_scatter | solution.py:55
  465.4 1.5 copy.20
  (11 shorter events, 0.2 us)
Async XLA Ops:
  37.1 6.7 %copy-start.1 = (s32[128]{0:T(128)S(1)}, s32[128]{0:T(128)}, u32[]{:S(2)}) copy-start(s32[128]{0:T(128)} %param.7) | copy-start | bytes 1540
  37.1 190.6 %all-to-all-start = ((f32[4,1,524288]{2,1,0:T(1,128)}), f32[4,1,524288]{2,1,0:T(1,128)}, u32[]{:S(2)}, u32[]{:S(2)}) async-start(f32[4,1,524288]{2,1,0:T(1,128)} %reshape.145), calls=%async_computation | async-start | bytes 16777216 | tf_op jit(solution)/shard_map/all_to_all | solution.py:45
  320.9 10.7 %copy-start.2 = (s32[8]{0:T(128)S(1)}, s32[8]{0:T(128)}, u32[]{:S(2)}) copy-start(s32[8]{0:T(128)} %param.6) | copy-start | bytes 100
  320.9 11.3 %copy-start = (f32[1024]{0:T(1024)S(1)}, f32[1024]{0:T(1024)}, u32[]{:S(2)}) copy-start(f32[1024]{0:T(1024)} %param.5) | copy-start | bytes 12292
  326.5 97.7 %all-to-all-start.1 = ((f32[128,32,256]{2,1,0:T(8,128)}), f32[128,32,256]{2,1,0:T(8,128)}, u32[]{:S(2)}, u32[]{:S(2)}) async-start(f32[128,32,256]{2,1,0:T(8,128)} %bitcast.42), calls=%async_computation.1 | async-start | bytes 8388608 | tf_op jit(solution)/shard_map/all_to_all | solution.py:51
  331.3 134.0 %reduce-scatter.2.cloned.1.call-start = ((), (), s32[]{:S(2)}) async-start(), calls=%async_computation.3 | async-start | bytes 589824 | tf_op jit(solution)/shard_map/reduce_scatter | solution.py:55
Sparse Core Ops, SparseCore 0:
  432.3 33.0 reduce-scatter.1
where the time goes:
time: 480 us; the launch traced here: 474 us
  waiting for transfers between devices  308 us (64%)
  local copies, waits for them, and re-layouts  80.7 us (17%)
  other arithmetic  30.2 us (6%)
  matrix products  29.9 us (6%)
  between operations  13.8 us (3%)
  starting transfers between devices  11.6 us (2%)
    all_to_all x1, waiting for transfers between devices, on_device(): lax.all_to_all(pressure, 'sec', split_axis=2, concat_axis=1, tiled=True)  183 us
    all_to_all x1, waiting for transfers between devices, on_device(): lax.all_to_all(modal, 'sec', split_axis=0, concat_axis=2, tiled=True)  91.3 us
    unnamed x9, local copies, waits for them, and re-layouts  47.3 us
    reduce_scatter x1, waiting for transfers between devices, on_device(): lax.psum_scatter(local_gram, ('tile', 'role'), scatter_dimension=1, tiled...  33.2 us
    all_to_all x1, other arithmetic, on_device(): lax.all_to_all(pressure, 'sec', split_axis=2, concat_axis=1, tiled=True)  28.8 us
    all_to_all x3, local copies, waits for them, and re-layouts, on_device(): lax.all_to_all(pressure, 'sec', split_axis=2, concat_axis=1, tiled=True)  21.9 us
    dot_general x1, matrix products, on_device(): jnp.einsum('okiq,ifqc->kofc', atab, split, precision=hi)  17.4 us
  transfers between devices with their start and end apart: 3, of which 3 were waited for; matrix products, arithmetic and copies ran while one was open for 0% of the time, Pallas kernels for 0%

commit v1 on v0

--- a/solution.py
+++ b/solution.py
@@ -42,7 +42,10 @@
     total_cells = group_cells * n_grp
     htab = time_table(snaps)
     atab = angle_table(mode_order, angles)
-    arrived = lax.all_to_all(pressure, "sec", split_axis=2, concat_axis=1, tiled=True)
+    arrived = jnp.concatenate(
+        lax.all_to_all(jnp.stack(jnp.split(pressure, lax.axis_size("sec"), axis=2)), "sec", 0, 0),
+        axis=1,
+    )
     spectra = jnp.einsum("rt,tqc->rqc", htab, arrived, precision=hi)
     split = spectra.reshape(2, half, angles, cell_dev)
     modal = jnp.einsum("okiq,ifqc->kofc", atab, split, precision=hi).reshape(modes, snaps, cell_dev)

time: 480 us -> 392 us (0.82); the launches traced: 474 us -> 392 us
  local copies, waits for them, and re-layouts: 80.7 us -> 19.5 us
  other arithmetic: 30.2 us -> 4.98 us
    unnamed x9 -> x6, local copies, waits for them, and re-layouts: 47.3 us -> 0.01 us
    all_to_all x1 -> x0, other arithmetic: 28.8 us -> none  [on_device(): lax.all_to_all(pressure, 'sec', split_axis=2, concat_axis=1, tiled=True)]
    all_to_all x3 -> x1, local copies, waits for them, and re-layouts: 21.9 us -> 3.99 us  [on_device(): lax.all_to_all(jnp.stack(jnp.split(pressure, lax.axis_size('sec'), axis=2...]
  transfers between devices with their start and end apart: 3 -> 3, of which waited for: 3 -> 3; matrix products, arithmetic and copies ran while one was open for 0% -> 1% of each run, Pallas kernels for 0% -> 0%
where the time goes in v1:
time: 392 us
  waiting for transfers between devices  308 us (79%)
  matrix products  34.2 us (9%)
  local copies, waits for them, and re-layouts  19.5 us (5%)
  between operations  13.5 us (3%)
  starting transfers between devices  11.7 us (3%)
  other arithmetic  4.98 us (1%)
    all_to_all x1, waiting for transfers between devices, on_device(): lax.all_to_all(jnp.stack(jnp.split(pressure, lax.axis_size('sec'), axis=2...  183 us
    all_to_all x1, waiting for transfers between devices, on_device(): lax.all_to_all(modal, 'sec', split_axis=0, concat_axis=2, tiled=True)  91.4 us
    reduce_scatter x1, waiting for transfers between devices, on_device(): lax.psum_scatter(local_gram, ('tile', 'role'), scatter_dimension=1, tiled...  33.2 us
    dot_general x1, matrix products, on_device(): jnp.einsum('okiq,ifqc->kofc', atab, split, precision=hi)  17.3 us
    dot_general x1, matrix products, on_device(): spectra = jnp.einsum('rt,tqc->rqc', htab, arrived, precision=hi)  12.8 us
  transfers between devices with their start and end apart: 3, of which 3 were waited for; matrix products, arithmetic and copies ran while one was open for 1% of the time, Pallas kernels for 0%

profile of v1, /device:TPU:0, one launch (start us, length us, event | category | flops | bytes accessed | tf_op | source)
XLA Modules:
  0.0 391.8 jit_solution(8651425654973589464)
XLA Ops:
  6.5 4.1 %slice_bitcast_fusion.3 = (f32[1,32,64,256]{3,2,1,0:T(8,128)S(1)}, f32[1,32,64,256]{3,2,1,0:T(8,128)S(1)}, f32[1,32,64,256]{3,2,1,0:T(8,128)S(1)}, f32[1,32,64,256]{3,2,1,0:T(8,128)S(1)}) fusion(f32[32,64,1024]{2,1,0:T(8,128)} %param.4), kind=kLoop, calls=%fused_computation.14 | loop fusion | bytes 16777216 | tf_op jit(solution)/shard_map/stack | solution.py:46
  10.7 3.5 pad_maximum_fusion
  14.2 6.5 %all-to-all-start = ((f32[4,32,64,256]{3,2,1,0:T(8,128)}), f32[4,32,64,256]{3,2,1,0:T(8,128)}, u32[]{:S(2)}, u32[]{:S(2)}) async-start(f32[4,32,64,256]{3,2,1,0:T(8,128)} %pad_maximum_fusion), calls=%async_computation | async-start | bytes 16777216 | tf_op jit(solution)/shard_map/all_to_all | solution.py:46
  20.8 0.1 sine_multiply_fusion.1
  20.9 0.0 copy-done.1
  20.9 0.6 sine_multiply_fusion
  21.5 183.2 %all-to-all-done = f32[4,32,64,256]{3,2,1,0:T(8,128)} async-done(((f32[4,32,64,256]{3,2,1,0:T(8,128)}), f32[4,32,64,256]{3,2,1,0:T(8,128)}, u32[]{:S(2)}, u32[]{:S(2)}) %all-to-all-start) | async-done | bytes 8388640 | tf_op jit(solution)/shard_map/all_to_all | solution.py:46
  204.8 4.0 %copy.7 = f32[4,32,64,256]{3,2,0,1:T(8,128)S(1)} copy(f32[4,32,64,256]{3,2,1,0:T(8,128)} %all-to-all-done) | data formatting | bytes 16777216 | tf_op jit(solution)/shard_map/all_to_all | solution.py:46
  208.8 12.8 %fusion.7 = f32[2,16,256,256,1]{3,1,2,0,4:T(8,128)S(1)} fusion(f32[2,16,32,1]{2,1,3,0:T(8,128)S(1)} %bitcast.47, f32[32,256,256]{2,1,0:T(8,128)S(1)} %bitcast.45), kind=kOutput, calls=%fused_computation.8 | convolution fusion | flops 805306368 | bytes 16781312 | tf_op jit(solution)/shard_map/rt,tqc->rqc/dot_general | solution.py:49
  221.6 17.3 %fusion.10 = f32[128,2,16,256]{0,3,1,2:T(8,128)} fusion(f32[2,16,256,256,1]{3,1,2,0,4:T(8,128)S(1)} %fusion.7, f32[1,128,2,256]{3,1,2,0:T(8,128)S(1)} %get-tuple-element.10, f32[1,128,2,256]{3,1,2,0:T(8,128)S(1)} %get-tuple-element.9), kind=kOutput, calls=%fused_computation.9 | convolution fusion | flops 6442582016 | bytes 13107200 | tf_op jit(solution)/shard_map/okiq,ifqc->kofc/dot_general | solution.py:51
  238.9 5.5 %copy.10 = f32[128,2,16,256]{3,2,1,0:T(8,128)} copy(f32[128,2,16,256]{0,3,1,2:T(8,128)} %fusion.10) | data formatting | bytes 8388608 | tf_op jit(solution)/shard_map/okiq,ifqc->kofc/transpose | solution.py:51
  244.4 5.0 %all-to-all-start.1 = ((f32[128,32,256]{2,1,0:T(8,128)}), f32[128,32,256]{2,1,0:T(8,128)}, u32[]{:S(2)}, u32[]{:S(2)}) async-start(f32[128,32,256]{2,1,0:T(8,128)} %bitcast.46), calls=%async_computation.1 | async-start | bytes 8388608 | tf_op jit(solution)/shard_map/all_to_all | solution.py:54
  249.4 0.3 reduce-scatter.2.cloned.1.call-start
  249.7 0.0 copy-done.2
  249.7 0.6 dynamic_slice.3
  250.3 0.0 copy-done
  250.3 0.6 multiply_select_fusion
  250.9 91.4 %all-to-all-done.1 = f32[128,32,256]{2,1,0:T(8,128)} async-done(((f32[128,32,256]{2,1,0:T(8,128)}), f32[128,32,256]{2,1,0:T(8,128)}, u32[]{:S(2)}, u32[]{:S(2)}) %all-to-all-start.1) | async-done | bytes 4194336 | tf_op jit(solution)/shard_map/all_to_all | solution.py:54
  342.3 2.7 copy.19
  345.0 4.1 %fusion.5 = f32[32,32,32]{2,1,0:T(8,128)S(1)} fusion(f32[32,32,1024]{2,1,0:T(8,128)S(1)} %bitcast.44, f32[1024]{0:T(1024)S(1)} %multiply_select_fusion), kind=kOutput, calls=%fused_computation.6 | convolution fusion | flops 403701760 | bytes 4329472 | tf_op jit(solution)/shard_map/kac,kbc->kab/dot_general | solution.py:57
  349.1 1.1 copy.12
  350.2 0.0 reduce-scatter.2.cloned.1.call-update
  350.2 33.2 %reduce-scatter.2.cloned.1.call-done = f32[32,4,32]{2,0,1:T(8,128)} async-done(((f32[32,32,32]{2,0,1:T(8,128)}), f32[32,4,32]{2,0,1:T(8,128)}) %reduce-scatter.2.cloned.1.call-update) | async-done | bytes 16400 | tf_op jit(solution)/shard_map/reduce_scatter | solution.py:58
  383.4 1.5 copy.13
  (7 shorter events, 0.1 us)
Async XLA Ops:
  14.2 6.7 %copy-start.1 = (s32[128]{0:T(128)S(1)}, s32[128]{0:T(128)}, u32[]{:S(2)}) copy-start(s32[128]{0:T(128)} %param.7) | copy-start | bytes 1540
  14.2 190.6 %all-to-all-start = ((f32[4,32,64,256]{3,2,1,0:T(8,128)}), f32[4,32,64,256]{3,2,1,0:T(8,128)}, u32[]{:S(2)}, u32[]{:S(2)}) async-start(f32[4,32,64,256]{3,2,1,0:T(8,128)} %pad_maximum_fusion), calls=%async_computation | async-start | bytes 16777216 | tf_op jit(solution)/shard_map/all_to_all | solution.py:46
  244.4 5.3 %copy-start.2 = (s32[8]{0:T(128)S(1)}, s32[8]{0:T(128)}, u32[]{:S(2)}) copy-start(s32[8]{0:T(128)} %param.6) | copy-start | bytes 100
  244.4 5.9 %copy-start = (f32[1024]{0:T(1024)S(1)}, f32[1024]{0:T(1024)}, u32[]{:S(2)}) copy-start(f32[1024]{0:T(1024)} %param.5) | copy-start | bytes 12292
  244.4 97.9 %all-to-all-start.1 = ((f32[128,32,256]{2,1,0:T(8,128)}), f32[128,32,256]{2,1,0:T(8,128)}, u32[]{:S(2)}, u32[]{:S(2)}) async-start(f32[128,32,256]{2,1,0:T(8,128)} %bitcast.46), calls=%async_computation.1 | async-start | bytes 8388608 | tf_op jit(solution)/shard_map/all_to_all | solution.py:54
  249.4 134.0 %reduce-scatter.2.cloned.1.call-start = ((), (), s32[]{:S(2)}) async-start(), calls=%async_computation.3 | async-start | bytes 589824 | tf_op jit(solution)/shard_map/reduce_scatter | solution.py:58
Sparse Core Ops, SparseCore 0:
  350.3 33.0 reduce-scatter.1
